TPU v7x, 256 devices: a whole 4x4x8 slice. The times are simulated.
256 devices in a mesh: feat: 16 (over y_lo, x, core), batch: 16 (over y_hi, z).
Axes of the slice: x: 4, y: 4 (y_hi: 2, y_lo: 2; y = y_hi * 2 + y_lo), z: 8, core: 2. Of those that a mesh axis runs over, the one named last changes fastest.
Arguments:
- features: bfloat16 [131072, 4096], P('batch', 'feat'), may hold values from -6 to 6
- src_tile: int32 [256, 2], P('batch'), may hold values from 0 to 7
- rel_type: int32 [256, 2], P('batch'), may hold values from 0 to 3
- timestamps: int32 [32768], P(('batch', 'feat')), may hold values from 0 to 127
- edge_tiles: bfloat16 [4, 128, 1024], replicated, may hold values from -0.1875 to 0.1875
- rel_weight: bfloat16 [4, 4096, 512], P(None, 'feat'), may hold values from -0.09375 to 0.09375
- attn_gain: float32 [512], replicated, may hold values from 0.1 to 1.9
- w_qkv: bfloat16 [512, 1536], replicated, as said below
- w_out: bfloat16 [512, 512], replicated, may hold values from -0.25 to 0.25
- cotangent: bfloat16 [32768, 512], P(('batch', 'feat')), may hold values from -96 to 96
Outputs:
- layer_out: bfloat16 [32768, 512], P(('batch', 'feat'))
- grad_qkv: bfloat16 [512, 1536], replicated
- grad_out: bfloat16 [512, 512], replicated
- grad_gain: bfloat16 [512], replicated
- grad_rel: bfloat16 [4, 4096, 512], P(None, 'feat')
Inputs may be any that keep to these rules, and one draw needn't show every extreme that they name: `src_tile`: index of a source tile within the batch group. `w_qkv`: query, key and value columns in that order along the second dimension.
All inputs are finite; a program needn't handle non-finite values.
Results may differ from a plain program's by a relative error of at most 0.014.
Values may be sent and summed in bfloat16 or wider, within the bound.
No kernel may reach another device: no remote copies, remote signals or barrier semaphores. Data moves between devices by JAX's collectives and lax.ppermute only.
A program may use at most 128 MiB of HBM per device.

v0:
```python
import functools

import jax
import jax.numpy as jnp
from jax import lax
from jax.experimental import pallas as pl
from jax.experimental.pallas import tpu as pltpu
from jax.sharding import Mesh
from jax.sharding import PartitionSpec as P

D = 512
HEADS = 8
HEAD_DIM = 64
NREL = 4
SLOTS = 2
TBLK = 128
SBLK = 1024
TILES = 8
PAIRS = 8
QUADS = 4
COLS = 256
HALF = 64
EPS = 1e-06

BF16 = jnp.bfloat16
F32 = jnp.float32


FEAT8 = ("fy", "fx")
SMEM = pl.BlockSpec(memory_space=pltpu.SMEM)
VMEM = pl.BlockSpec(memory_space=pltpu.VMEM)
HBM = pl.BlockSpec(memory_space=pltpu.MemorySpace.HBM)

SRC, REL, PLACE = 0, SLOTS, 2 * SLOTS
CORE, X, BY = 0, 1, 2


def dot(a, b, ca, cb):
    return lax.dot_general(a, b, (((ca,), (cb,)), ((), ())), preferred_element_type=F32)


def forward_kernel(table, feats, edges, weight, combos, keep, send, tiles, edge, weights, products, proj, sems):
    def tile_copy(t):
        return pltpu.make_async_copy(feats.at[pl.ds(t * SBLK, SBLK)], tiles.at[t], sems.at[t])

    edge_copy = pltpu.make_async_copy(edges, edge, sems.at[TILES])
    weight_copy = pltpu.make_async_copy(weight, weights, sems.at[TILES + 1])
    edge_copy.start()
    tile_copy(0).start()
    edge_copy.wait()
    tile_copy(1).start()
    for t in range(TILES):
        tile_copy(t).wait()
        if t + 2 < TILES:
            tile_copy(t + 2).start()
        elif t + 2 == TILES:
            weight_copy.start()
        both = dot(edge[...], tiles[t], 1, 0).astype(BF16)
        for r in range(NREL):
            products[r, t] = both[r * TBLK : (r + 1) * TBLK]
    out_copy = pltpu.make_async_copy(products, combos, sems.at[TILES + 2])
    out_copy.start()
    weight_copy.wait()
    for r in range(NREL):
        rows = products[r].reshape(TILES * TBLK, COLS)
        proj[r * TILES : (r + 1) * TILES] = dot(rows, weights[r], 1, 0).reshape(TILES, TBLK, D)
    mine = table[PLACE, CORE]
    for j in range(PAIRS):
        for out, which in ((send, 1 - mine), (keep, mine)):
            b = 2 * j + which
            first = proj[table[REL, b] * TILES + table[SRC, b]]
            second = proj[table[REL + 1, b] * TILES + table[SRC + 1, b]]
            out[j] = (first + second).astype(BF16)
    out_copy.wait()


def forward(table, features, edges, weight):
    return pl.pallas_call(
        forward_kernel,
        in_specs=[SMEM, HBM, HBM, HBM],
        out_specs=[HBM, VMEM, VMEM],
        out_shape=[
            jax.ShapeDtypeStruct((NREL, TILES, TBLK, COLS), BF16),
            jax.ShapeDtypeStruct((PAIRS, TBLK, D), BF16),
            jax.ShapeDtypeStruct((PAIRS, TBLK, D), BF16),
        ],
        scratch_shapes=[
            pltpu.VMEM((TILES, SBLK, COLS), BF16),
            pltpu.VMEM((NREL * TBLK, SBLK), BF16),
            pltpu.VMEM((NREL, COLS, D), BF16),
            pltpu.VMEM((NREL, TILES, TBLK, COLS), BF16),
            pltpu.VMEM((NREL * TILES, TBLK, D), F32),
            pltpu.SemaphoreType.DMA((TILES + 3,)),
        ],
        compiler_params=pltpu.CompilerParams(vmem_limit_bytes=51 * 2**20),
        cost_estimate=pl.CostEstimate(flops=3 * 2**30, bytes_accessed=10 * 2**20, transcendentals=0),
        name="forward",
    )(table, features, edges, weight)


def stacked(pair, low):
    zero = jnp.zeros_like(pair)
    return jnp.concatenate([jnp.where(low, pair, zero), jnp.where(low, zero, pair)], axis=0)


def side_by_side(both):
    half = both.shape[0] // 2
    return jnp.concatenate([both[:half], both[half:]], axis=1)


def layer_kernel(arrived, times, gain, w_qkv, w_out, cot, out, d_total, normed_out, d_projected_out, context_out):
    total = arrived[0].astype(F32)
    for j in range(1, PAIRS):
        total = total + arrived[j].astype(F32)
    sigma = 1.0 / (1.0 + jnp.exp(-total))
    tokens = (total * sigma).astype(BF16).astype(F32)
    mean = jnp.mean(tokens * tokens, axis=1, keepdims=True)
    scale = lax.rsqrt(mean + EPS)
    scaled = tokens * scale
    gains = gain[...]
    normed = (scaled * gains).astype(BF16)
    projected = dot(normed, w_qkv[...], 1, 0).astype(BF16)

    row_time = jnp.broadcast_to(times[...], (TBLK, TBLK))
    allowed = row_time <= row_time.T
    allowed = jnp.concatenate([allowed.astype(F32)] * 2, axis=0) > 0.5
    low = lax.broadcasted_iota(jnp.int32, (TBLK, 2 * HEAD_DIM), 1) < HEAD_DIM
    inv = 1.0 / (HEAD_DIM**0.5)

    cots = cot[...]
    d_context = dot(cots, w_out[...], 1, 1).astype(BF16)
    contexts = []
    d_q, d_k, d_v = [], [], []
    for h in range(HEADS // 2):
        at = slice(2 * HEAD_DIM * h, 2 * HEAD_DIM * (h + 1))
        q = projected[:, at]
        k = projected[:, D + at.start : D + at.stop]
        v = projected[:, 2 * D + at.start : 2 * D + at.stop]
        q2, k2, v2 = stacked(q, low), stacked(k, low), stacked(v, low)
        scores = dot(q2, k, 1, 1) * inv
        scores = jnp.where(allowed, scores, -1e30)
        top = jnp.max(scores, axis=1, keepdims=True)
        expo = jnp.exp(scores - top)
        soft = expo / jnp.sum(expo, axis=1, keepdims=True)
        weights = soft.astype(BF16)
        contexts.append(dot(side_by_side(weights), v2, 1, 0).astype(BF16))
        dc2 = stacked(d_context[:, at], low)
        d_weights = dot(dc2, v, 1, 1).astype(BF16).astype(F32)
        d_v.append(dot(weights, dc2, 0, 0).astype(BF16))
        d_soft = soft * (d_weights - jnp.sum(d_weights * soft, axis=1, keepdims=True))
        d_scores = (jnp.where(allowed, d_soft, 0.0) * inv).astype(BF16)
        d_q.append(dot(side_by_side(d_scores), k2, 1, 0).astype(BF16))
        d_k.append(dot(d_scores, q2, 0, 0).astype(BF16))
    context = jnp.concatenate(contexts, axis=1)
    out[...] = (tokens + dot(context, w_out[...], 1, 0)).astype(BF16)

    d_projected = jnp.concatenate(d_q + d_k + d_v, axis=1)
    d_normed = dot(d_projected, w_qkv[...], 1, 1).astype(BF16).astype(F32)
    d_gain = jnp.sum(d_normed * scaled, axis=0, keepdims=True)
    inner = d_normed * gains
    along = jnp.sum(inner * tokens, axis=1, keepdims=True)
    d_tokens = cots.astype(F32) + inner * scale - tokens * (scale * scale * scale * along * (1.0 / D))
    slope = sigma * (1.0 + total * (1.0 - sigma))
    d_total[:TBLK] = (d_tokens.astype(BF16).astype(F32) * slope).astype(BF16)
    high = d_gain.astype(BF16).astype(F32)
    row = lax.broadcasted_iota(jnp.int32, (8, D), 0)
    both = jnp.where(row == 0, high, jnp.where(row == 1, d_gain - high, 0.0))
    d_total[TBLK:] = both.astype(BF16)

    normed_out[...] = normed
    d_projected_out[...] = d_projected
    context_out[...] = context


def layer(arrived, times, gain, w_qkv, w_out, cot):
    return pl.pallas_call(
        layer_kernel,
        in_specs=[VMEM] * 6,
        out_specs=[VMEM] * 5,
        out_shape=[
            jax.ShapeDtypeStruct((TBLK, D), BF16),
            jax.ShapeDtypeStruct((TBLK + 8, D), BF16),
            jax.ShapeDtypeStruct((TBLK, D), BF16),
            jax.ShapeDtypeStruct((TBLK, 3 * D), BF16),
            jax.ShapeDtypeStruct((TBLK, D), BF16),
        ],
        compiler_params=pltpu.CompilerParams(vmem_limit_bytes=16 * 2**20),
        cost_estimate=pl.CostEstimate(flops=2**30, bytes_accessed=8 * 2**20, transcendentals=2**18),
        name="layer",
    )(arrived, times, gain, w_qkv, w_out, cot)


def terms_kernel(table, normed, d_projected, context, cot, keep, send, terms):
    d_qkv = dot(normed[...], d_projected[...], 0, 0).astype(BF16)
    d_out = dot(context[...], cot[...], 0, 0).astype(BF16)
    for part in range(4):
        source = d_qkv[:, part * D : (part + 1) * D] if part < 3 else d_out
        source = source.reshape(2 * QUADS, 2, 32, D)
        for half in range(2):
            terms[:, 2 * part + half] = source[:, half]
    mine = table[PLACE, CORE]
    keep[...] = terms[pl.ds(mine * QUADS, QUADS)]
    send[...] = terms[pl.ds((1 - mine) * QUADS, QUADS)]


def weight_terms(table, normed, d_projected, context, cot):
    terms = (QUADS, 8, 32, D)
    return pl.pallas_call(
        terms_kernel,
        in_specs=[SMEM] + [VMEM] * 4,
        out_specs=[VMEM] * 2,
        out_shape=[jax.ShapeDtypeStruct(terms, BF16), jax.ShapeDtypeStruct(terms, BF16)],
        scratch_shapes=[pltpu.VMEM((2 * QUADS, 8, 32, D), BF16)],
        compiler_params=pltpu.CompilerParams(vmem_limit_bytes=16 * 2**20),
        cost_estimate=pl.CostEstimate(flops=2**28, bytes_accessed=5 * 2**20, transcendentals=0),
        name="terms",
    )(table, normed, d_projected, context, cot)


def relations_kernel(first, table, own, other, combos, keep, send, gains, summed, rows):
    mine = table[PLACE, CORE]
    half = pl.multiple_of(table[PLACE, BY] * HALF, HALF)
    rest = pl.multiple_of(HALF - half, HALF)

    near = jnp.zeros((8, D), F32)
    far = jnp.zeros((8, D), F32)
    for j in range(PAIRS):
        near = near + own[j, TBLK:].astype(F32)
        far = far + other[j, TBLK:].astype(F32)
    gains[...] = near + far

    def one_relation(i, _):
        summed[...] = jnp.zeros_like(summed)
        for j in range(PAIRS):
            for ref, which in ((own, mine), (other, 1 - mine)):
                b = 2 * j + which
                for slot in range(SLOTS):

                    @pl.when(table[REL + slot, b] == first + i)
                    def _():
                        at = table[SRC + slot, b]
                        summed[at] = summed[at] + ref[j, :TBLK].astype(F32)

        sums = summed[...].astype(BF16).reshape(TILES * TBLK, D)
        rows[...] = dot(combos[first + i], sums, 1, 0).astype(BF16).reshape(2, TBLK, D)
        keep[pl.ds(2 * i, 2)] = rows[:, pl.ds(half, HALF)]
        send[pl.ds(2 * i, 2)] = rows[:, pl.ds(rest, HALF)]
        return 0

    lax.fori_loop(0, NREL // 2, one_relation, 0)


def relations_grad(first, table, own, other, combos):
    return pl.pallas_call(
        functools.partial(relations_kernel, first),
        in_specs=[SMEM] + [VMEM] * 3,
        out_specs=[VMEM] * 3,
        out_shape=[
            jax.ShapeDtypeStruct((4, HALF, D), BF16),
            jax.ShapeDtypeStruct((4, HALF, D), BF16),
            jax.ShapeDtypeStruct((8, D), F32),
        ],
        scratch_shapes=[pltpu.VMEM((TILES, TBLK, D), F32), pltpu.VMEM((2, TBLK, D), BF16)],
        compiler_params=pltpu.CompilerParams(vmem_limit_bytes=14 * 2**20),
        cost_estimate=pl.CostEstimate(flops=2**29, bytes_accessed=6 * 2**20, transcendentals=0),
        name="relations",
    )(table, own, other, combos)


def assemble_kernel(table, *refs):
    own, other, (grad_qkv, grad_out) = refs[:QUADS], refs[QUADS : 2 * QUADS], refs[2 * QUADS :]
    for k in range(QUADS):
        x = lax.rem(table[PLACE, X] + 4 - k, 4)
        for ref, which in ((own[k], table[PLACE, CORE]), (other[k], 1 - table[PLACE, CORE])):
            first = (which * QUADS + x) * 64
            for piece in range(8):
                rows = pl.ds(pl.multiple_of(first + (piece % 2) * 32, 32), 32)
                part = piece // 2
                target, at = (grad_qkv, part * D) if part < 3 else (grad_out, 0)
                target[rows, at : at + D] = ref[piece]


def assemble(table, own, other):
    return pl.pallas_call(
        assemble_kernel,
        in_specs=[SMEM] + [VMEM] * (2 * QUADS),
        out_specs=[VMEM, VMEM],
        out_shape=[jax.ShapeDtypeStruct((D, 3 * D), BF16), jax.ShapeDtypeStruct((D, D), BF16)],
        compiler_params=pltpu.CompilerParams(vmem_limit_bytes=12 * 2**20),
        cost_estimate=pl.CostEstimate(flops=0, bytes_accessed=4 * 2**20, transcendentals=0),
        name="assemble",
    )(table, *own, *other)


def swap(x, axis):
    return lax.ppermute(x, axis, [(0, 1), (1, 0)])


def exchange(pieces, axes):
    return lax.all_to_all(pieces, axes, split_axis=0, concat_axis=0, tiled=True)


def gather(x, axes):
    devices = lax.axis_size(axes)
    return exchange(jnp.broadcast_to(x[None], (devices, *x.shape)), axes)


def to_x(x, k):
    return lax.ppermute(x, "fx", [(i, (i + k) % 4) for i in range(4)])


def added(x, y):
    return (x.astype(F32) + y.astype(F32)).astype(BF16)


def summed(x):
    return x.astype(F32).sum(axis=0)


def after(x, first):
    return lax.optimization_barrier((x, first))[0]


def shards(features, src, rel, timestamps, edge_tiles, rel_weight, attn_gain, w_qkv, w_out, cotangent):
    by = lax.axis_index("by")
    lane = lax.broadcasted_iota(jnp.int32, (1, src.shape[0]), 1)
    place = jnp.where(lane == X, lax.axis_index("fx"), by)
    place = jnp.where(lane == CORE, lax.axis_index("fc"), place).astype(jnp.int32)
    table = jnp.concatenate([src.T, rel.T, place], axis=0)
    combos, keep, send = forward(table, features, edge_tiles.reshape(NREL * TBLK, SBLK), rel_weight)
    arrived = exchange(added(keep, swap(send, "fc")), FEAT8)

    layer_out, d_total, normed, d_projected, context = layer(
        arrived, timestamps.reshape(1, TBLK), attn_gain.reshape(1, D), w_qkv, w_out, cotangent
    )

    own = gather(d_total, FEAT8)
    keep, send = weight_terms(table, normed, d_projected, context, cotangent)
    terms = added(keep, swap(send, "fc"))
    turned = jnp.swapaxes(combos.reshape(NREL, TILES * TBLK, COLS), 1, 2)
    own, terms, turned = lax.optimization_barrier((own, terms, turned))
    terms = exchange(terms, "fx")
    other = swap(own, "fc")
    keep, send, gains = relations_grad(0, table, own, other, turned)
    got = swap(send, "by")
    keep2, send2, _ = relations_grad(NREL // 2, table, own, other, turned)
    rel_terms = jnp.concatenate([added(keep, got), added(keep2, swap(send2, "by"))], axis=0)

    terms = summed(after(terms, keep2)).astype(BF16)
    gain = gains[0:1] + gains[1:2]
    high = gain.astype(BF16)
    low = (gain - high.astype(F32)).astype(BF16)
    gain_rows = jnp.concatenate([high, low, jnp.zeros((6, D), BF16)], axis=0)
    gain_rows = jnp.broadcast_to(gain_rows[None], (8, 8, D))

    piece = summed(exchange(jnp.concatenate([rel_terms, terms, gain_rows], axis=1), "bz")).astype(BF16)
    aside = piece[HALF:]
    partner = swap(aside, "by").astype(F32)
    beside = swap(aside[:32], "fy").astype(F32)
    across = lax.ppermute(aside[:32], ("fy", "by"), [(i, 3 - i) for i in range(4)]).astype(F32)
    aside = aside.astype(F32)
    term = (aside[:32] + partner[:32]) + (beside + across)
    gain = aside[32:] + partner[32:]
    gain = jnp.broadcast_to(gain[0:1] + gain[1:2], (8, D))
    rows = gather(jnp.concatenate([piece[:HALF], term.astype(BF16), gain.astype(BF16)], axis=0), "bz")
    grad_gain = rows[0, HALF + 32]
    terms = rows[:, HALF : HALF + 32]

    piece = rows[:, :HALF]
    partner = swap(piece, "by")
    first, second = jnp.where(by == 0, piece, partner), jnp.where(by == 0, partner, piece)
    grad_rel = jnp.stack([first, second], axis=1).reshape(NREL, COLS, D)

    own = [terms] + [to_x(terms, k) for k in range(1, QUADS)]
    other = [swap(part, "fc") for part in own]
    grad_qkv, grad_out = assemble(table, own, other)
    return (layer_out, grad_qkv, grad_out, grad_gain, grad_rel)


def solution(mesh):
    split = Mesh(mesh.devices.reshape(2, 4, 2, 2, 8), ("fy", "fx", "fc", "by", "bz"))
    feat = ("fy", "fx", "fc")
    batch = ("by", "bz")
    in_specs = (
        P(batch, feat),
        P(batch, None),
        P(batch, None),
        P(batch + feat),
        P(),
        P(None, feat, None),
        P(),
        P(),
        P(),
        P(batch + feat, None),
    )
    out_specs = (P(batch + feat, None), P(), P(), P(), P(None, feat, None))
    return jax.shard_map(shards, mesh=split, in_specs=in_specs, out_specs=out_specs, check_vma=False)
```

profile of v0, /device:TPU:16, one launch (start us, length us, event | category | flops | bytes accessed | tf_op | source)
XLA Modules:
  0.0 172.1 jit_solution(4272283670600354596)
XLA Ops:
  1.4 9.5 %forward.1 = (bf16[4,8,128,256]{3,2,1,0:T(8,128)(2,1)}, bf16[8,128,512]{2,1,0:T(8,128)(2,1)S(1)}, bf16[8,128,512]{2,1,0:T(8,128)(2,1)S(1)}) custom-call(s32[5,16]{1,0:T(8,128)S(1)} %pad_add_fusion.table, bf16[8192,256]{1,0:T(8,128)(2,1)} %feats.1, bf16[512,1024]{1,0:T(8,128)(2,1)} %bitcast.20, bf16[4,256,512]{2,1,0:T(8,128)(2,1)} %weight.1), custom_call_target="tpu_custom_call" | custom-call | flops 3221225472 | bytes 10485760 | tf_op jit(solution)/shard_map/forward/pallas_call | solution.py:78
  11.0 2.6 %collective-permute-done = bf16[8,128,512]{2,1,0:T(8,128)(2,1)S(1)} collective-permute-done((bf16[8,128,512]{2,1,0:T(8,128)(2,1)S(1)}, bf16[8,128,512]{2,1,0:T(8,128)(2,1)S(1)}, u32[]{:S(2)}, u32[]{:S(2)}) %collective-permute-start) | collective-permute-done | bytes 1048608 | tf_op jit(solution)/shard_map/ppermute | solution.py:296
  14.0 20.9 %all_to_all.25.arrived = bf16[8,128,512]{2,1,0:T(8,128)(2,1)S(1)} all-to-all(bf16[8,128,512]{2,1,0:T(8,128)(2,1)S(1)} %add_convert_fusion.1), channel_id=1, replica_groups=mesh['fy'=2,'fx'=4,'fc'=2,'by'=2,'bz'=8] {'fy','fx'}, dimensions={0} | all-to-all | bytes 2097152 | tf_op jit(solution)/shard_map/all_to_all | solution.py:300
  34.9 3.6 %layer.1 = (bf16[128,512]{1,0:T(8,128)(2,1)}, bf16[136,512]{1,0:T(8,128)(2,1)S(1)}, bf16[128,512]{1,0:T(8,128)(2,1)S(1)}, bf16[128,1536]{1,0:T(8,128)(2,1)S(1)}, bf16[128,512]{1,0:T(8,128)(2,1)S(1)}) custom-call(bf16[8,128,512]{2,1,0:T(8,128)(2,1)S(1)} %all_to_all.25.arrived, s32[1,128]{1,0:T(1,128)S(1)} %bitcast.15, f32[1,512]{1,0:T(1,128)S(1)} %bitcast.14, ...), custom_call_target="tpu_custom_call" | custom-call | flops 1073741824 | bytes 8388608 | tf_op jit(solution)/shard_map/layer/pallas_call | solution.py:176
  38.6 2.4 %terms.1 = (bf16[4,8,32,512]{3,2,1,0:T(8,128)(2,1)S(1)}, bf16[4,8,32,512]{3,2,1,0:T(8,128)(2,1)}) custom-call(s32[5,16]{1,0:T(8,128)S(1)} %pad_add_fusion.table, bf16[128,512]{1,0:T(8,128)(2,1)S(1)} %get-tuple-element.30.normed, bf16[128,1536]{1,0:T(8,128)(2,1)S(1)} %get-tuple-element.31.d_projected, bf16[128,512]{1,0:T(8,128)(2,1)S(1)} %get-tuple-element.32.context, ...), custom_call_target="tpu_custom_call" | custom-call | flops 268435456 | bytes 5242880 | tf_op jit(solution)/shard_map/terms/pallas_call | solution.py:208
  43.1 3.6 %all-to-all-start.1 = ((bf16[8,136,512]{2,1,0:T(8,128)(2,1)}), bf16[8,136,512]{2,1,0:T(8,128)(2,1)S(1)}, u32[]{:S(2)}, u32[]{:S(2)}) async-start(bf16[8,136,512]{2,1,0:T(8,128)(2,1)} %broadcast_in_dim.41), calls=%async_computation.1 | async-start | bytes 2228224 | tf_op jit(solution)/shard_map/all_to_all | solution.py:300
  46.6 3.0 %copy.18 = bf16[4,1024,256]{1,2,0:T(8,128)(2,1)S(1)} copy(bf16[4,1024,256]{2,1,0:T(8,128)(2,1)} %bitcast.16) | data formatting | bytes 4194304 | tf_op jit(solution)/shard_map/reshape | solution.py:340
  49.6 2.9 %add_convert_fusion = bf16[4,8,32,512]{3,2,1,0:T(8,128)(2,1)} fusion(bf16[4,8,32,512]{3,2,1,0:T(8,128)(2,1)} %collective-permute-done.1, bf16[4,8,32,512]{3,2,1,0:T(8,128)(2,1)} %copy-done), kind=kLoop, calls=%fused_computation | loop fusion | flops 2097152 | bytes 3145728 | tf_op jit(solution)/shard_map/convert_element_type | solution.py:313
  52.6 11.3 %all-to-all-done.1.own = bf16[8,136,512]{2,1,0:T(8,128)(2,1)S(1)} async-done(((bf16[8,136,512]{2,1,0:T(8,128)(2,1)}), bf16[8,136,512]{2,1,0:T(8,128)(2,1)S(1)}, u32[]{:S(2)}, u32[]{:S(2)}) %all-to-all-start.1) | async-done | bytes 1114144 | tf_op jit(solution)/shard_map/all_to_all | solution.py:300
  63.9 4.4 %all-to-all-start.2 = ((bf16[4,8,32,512]{3,2,1,0:T(8,128)(2,1)}), bf16[4,8,32,512]{3,2,1,0:T(8,128)(2,1)}, u32[]{:S(2)}, u32[]{:S(2)}) async-start(bf16[4,8,32,512]{3,2,1,0:T(8,128)(2,1)} %add_convert_fusion), calls=%async_computation.2 | async-start | bytes 2097152 | tf_op jit(solution)/shard_map/all_to_all | solution.py:300
  68.5 4.1 %relations.2 = (bf16[4,64,512]{2,1,0:T(8,128)(2,1)S(1)}, bf16[4,64,512]{2,1,0:T(8,128)(2,1)}, f32[8,512]{1,0:T(8,128)S(1)}) custom-call(s32[5,16]{1,0:T(8,128)S(1)} %pad_add_fusion.table, bf16[8,136,512]{2,1,0:T(8,128)(2,1)S(1)} %all-to-all-done.1.own, bf16[8,136,512]{2,1,0:T(8,128)(2,1)} %collective-permute-done.2.other, bf16[4,256,1024]{2,1,0:T(8,128)(2,1)S(1)} %bitcast.12), custom_call_target="tpu_custom_call" | custom-call | flops 536870912 | bytes 6291456 | tf_op jit(solution)/shard_map/relations/pallas_call | solution.py:254
  73.3 4.2 %relations.3 = (bf16[4,64,512]{2,1,0:T(8,128)(2,1)S(1)}, bf16[4,64,512]{2,1,0:T(8,128)(2,1)}, f32[8,512]{1,0:T(8,128)}) custom-call(s32[5,16]{1,0:T(8,128)S(1)} %pad_add_fusion.table, bf16[8,136,512]{2,1,0:T(8,128)(2,1)S(1)} %all-to-all-done.1.own, bf16[8,136,512]{2,1,0:T(8,128)(2,1)} %collective-permute-done.2.other, bf16[4,256,1024]{2,1,0:T(8,128)(2,1)S(1)} %bitcast.13), custom_call_target="tpu_custom_call" | custom-call | flops 536870912 | bytes 6291456 | tf_op jit(solution)/shard_map/relations/pallas_call | solution.py:254
  78.2 2.7 %collective-permute-start.4 = (bf16[4,64,512]{2,1,0:T(8,128)(2,1)}, bf16[4,64,512]{2,1,0:T(8,128)(2,1)S(1)}, u32[]{:S(2)}, u32[]{:S(2)}) collective-permute-start(bf16[4,64,512]{2,1,0:T(8,128)(2,1)} %get-tuple-element.41), channel_id=1, source_target_pairs={{0,8},{8,0},{1,9},{9,1},{2,10},{10,2},{3,11},{11,3},{4,12},{12,4},... | collective-permute-start | bytes 786440 | tf_op jit(solution)/shard_map/ppermute | solution.py:296
  81.0 3.3 %all-to-all-done.2 = bf16[4,8,32,512]{3,2,1,0:T(8,128)(2,1)} async-done(((bf16[4,8,32,512]{3,2,1,0:T(8,128)(2,1)}), bf16[4,8,32,512]{3,2,1,0:T(8,128)(2,1)}, u32[]{:S(2)}, u32[]{:S(2)}) %all-to-all-start.2) | async-done | bytes 1048608 | tf_op jit(solution)/shard_map/all_to_all | solution.py:300
  85.7 2.9 %collective-permute-done.4 = bf16[4,64,512]{2,1,0:T(8,128)(2,1)S(1)} collective-permute-done((bf16[4,64,512]{2,1,0:T(8,128)(2,1)}, bf16[4,64,512]{2,1,0:T(8,128)(2,1)S(1)}, u32[]{:S(2)}, u32[]{:S(2)}) %collective-permute-start.4) | collective-permute-done | bytes 262176 | tf_op jit(solution)/shard_map/ppermute | solution.py:296
  90.7 32.7 %all_to_all.26 = bf16[8,104,512]{2,1,0:T(8,128)(2,1)S(1)} all-to-all(bf16[8,104,512]{2,1,0:T(8,128)(2,1)S(1)} %pad_maximum_fusion.1), channel_id=1, replica_groups=mesh['fy'=2,'fx'=4,'fc'=2,'by'=2,'bz'=8] {'bz'}, dimensions={0} | all-to-all | bytes 1703936 | tf_op jit(solution)/shard_map/all_to_all | solution.py:300
  123.6 2.3 %collective-permute-start.5 = (bf16[40,512]{1,0:T(8,128)(2,1)S(1)}, bf16[40,512]{1,0:T(8,128)(2,1)S(1)}, u32[]{:S(2)}, u32[]{:S(2)}) collective-permute-start(bf16[40,512]{1,0:T(8,128)(2,1)S(1)} %get-tuple-element.50), channel_id=1, source_target_pairs={{0,8},{8,0},{1,9},{9,1},{2,10},{10,2},{3,11},{11,3},{4,12},{12,4},... | collective-permute-start | bytes 122888 | tf_op jit(solution)/shard_map/ppermute | solution.py:296
  130.4 24.0 %all_to_all.27 = bf16[8,104,512]{2,1,0:T(8,128)(2,1)S(1)} all-to-all(bf16[8,104,512]{2,1,0:T(8,128)(2,1)S(1)} %broadcast_in_dim.45), channel_id=1, replica_groups=mesh['fy'=2,'fx'=4,'fc'=2,'by'=2,'bz'=8] {'bz'}, dimensions={0} | all-to-all | bytes 1703936 | tf_op jit(solution)/shard_map/all_to_all | solution.py:300
  154.5 2.4 %collective-permute-start.15 = (bf16[8,64,512]{2,1,0:T(8,128)(2,1)S(1)}, bf16[8,64,512]{2,1,0:T(8,128)(2,1)S(1)}, u32[]{:S(2)}, u32[]{:S(2)}) collective-permute-start(bf16[8,64,512]{2,1,0:T(8,128)(2,1)S(1)} %slice.69), channel_id=1, source_target_pairs={{0,8},{8,0},{1,9},{9,1},{2,10},{10,2},{3,11},{11,3},{4,12},{12,4},... | collective-permute-start | bytes 1572872 | tf_op jit(solution)/shard_map/ppermute | solution.py:296
  158.2 2.7 %collective-permute-start.9 = (bf16[8,32,512]{2,1,0:T(8,128)(2,1)S(1)}, bf16[8,32,512]{2,1,0:T(8,128)(2,1)S(1)}, u32[]{:S(2)}, u32[]{:S(2)}) collective-permute-start(bf16[8,32,512]{2,1,0:T(8,128)(2,1)S(1)} %slice.67.refs_0_), channel_id=1, source_target_pairs={{0,64},{32,96},{64,0},{96,32},{1,65},{33,97},{65,1},{97,33},{2,66}... | collective-permute-start | bytes 786440 | tf_op jit(solution)/shard_map/ppermute | solution.py:309
  160.9 1.4 collective-permute-start.10
  162.9 1.7 collective-permute-done.8.refs_1_
  164.6 3.5 %collective-permute-done.9.refs_2_ = bf16[8,32,512]{2,1,0:T(8,128)(2,1)S(1)} collective-permute-done((bf16[8,32,512]{2,1,0:T(8,128)(2,1)S(1)}, bf16[8,32,512]{2,1,0:T(8,128)(2,1)S(1)}, u32[]{:S(2)}, u32[]{:S(2)}) %collective-permute-start.9) | collective-permute-done | bytes 262176 | tf_op jit(solution)/shard_map/ppermute | solution.py:309
  170.0 2.1 %assemble.1 = (bf16[512,1536]{1,0:T(8,128)(2,1)}, bf16[512,512]{1,0:T(8,128)(2,1)}) custom-call(s32[5,16]{1,0:T(8,128)S(1)} %pad_add_fusion.table, bf16[8,32,512]{2,1,0:T(8,128)(2,1)S(1)} %slice.67.refs_0_, bf16[8,32,512]{2,1,0:T(8,128)(2,1)S(1)} %collective-permute-done.8.refs_1_, bf16[8,32,512]{2,1,0:T(8,128)(2,1)S(1)} %collective-permute-done.9.refs_2_, ...), custom_call_target="tpu_custom_call" | custom-call | bytes 4194304 | tf_op jit(solution)/shard_map/assemble/pallas_call | solution.py:284
  (67 shorter events, 16.8 us)
Async XLA Ops:
  10.8 2.7 %collective-permute-start = (bf16[8,128,512]{2,1,0:T(8,128)(2,1)S(1)}, bf16[8,128,512]{2,1,0:T(8,128)(2,1)S(1)}, u32[]{:S(2)}, u32[]{:S(2)}) collective-permute-start(bf16[8,128,512]{2,1,0:T(8,128)(2,1)S(1)} %get-tuple-element.27), channel_id=1, source_target_pairs={{0,16},{16,0},{1,17},{17,1},{2,18},{18,2},{3,19},{19,3},{4,20},{20... | collective-permute-start | bytes 3145736 | tf_op jit(solution)/shard_map/ppermute | solution.py:296
  13.6 21.3 %copy-start.4 = (bf16[128,512]{1,0:T(8,128)(2,1)S(1)}, bf16[128,512]{1,0:T(8,128)(2,1)}, u32[]{:S(2)}) copy-start(bf16[128,512]{1,0:T(8,128)(2,1)} %cot.3) | copy-start | bytes 393220
  13.9 21.0 %copy-start.2 = (bf16[512,1536]{1,0:T(8,128)(2,1)S(1)}, bf16[512,1536]{1,0:T(8,128)(2,1)}, u32[]{:S(2)}) copy-start(bf16[512,1536]{1,0:T(8,128)(2,1)} %w_qkv.1) | copy-start | bytes 4718596
  13.9 21.0 %copy-start.3 = (bf16[512,512]{1,0:T(8,128)(2,1)S(1)}, bf16[512,512]{1,0:T(8,128)(2,1)}, u32[]{:S(2)}) copy-start(bf16[512,512]{1,0:T(8,128)(2,1)} %w_out.1) | copy-start | bytes 1572868
  13.9 21.0 %copy-start.5 = (f32[512]{0:T(512)S(1)}, f32[512]{0:T(512)}, u32[]{:S(2)}) copy-start(f32[512]{0:T(512)} %param.16) | copy-start | bytes 6148
  13.9 21.0 %copy-start.6 = (s32[128]{0:T(128)S(1)}, s32[128]{0:T(128)}, u32[]{:S(2)}) copy-start(s32[128]{0:T(128)} %param.13) | copy-start | bytes 1540
  41.0 1.0 copy-start
  42.0 7.6 %collective-permute-start.1 = (bf16[4,8,32,512]{3,2,1,0:T(8,128)(2,1)}, bf16[4,8,32,512]{3,2,1,0:T(8,128)(2,1)}, u32[]{:S(2)}, u32[]{:S(2)}) collective-permute-start(bf16[4,8,32,512]{3,2,1,0:T(8,128)(2,1)} %get-tuple-element.34), channel_id=1, source_target_pairs={{0,16},{16,0},{1,17},{17,1},{2,18},{18,2},{3,19},{19,3},{4,20},{20... | collective-permute-start | bytes 3145736 | tf_op jit(solution)/shard_map/ppermute | solution.py:296
  43.1 20.9 %all-to-all-start.1 = ((bf16[8,136,512]{2,1,0:T(8,128)(2,1)}), bf16[8,136,512]{2,1,0:T(8,128)(2,1)S(1)}, u32[]{:S(2)}, u32[]{:S(2)}) async-start(bf16[8,136,512]{2,1,0:T(8,128)(2,1)} %broadcast_in_dim.41), calls=%async_computation.1 | async-start | bytes 2228224 | tf_op jit(solution)/shard_map/all_to_all | solution.py:300
  63.9 4.5 %collective-permute-start.2 = (bf16[8,136,512]{2,1,0:T(8,128)(2,1)S(1)}, bf16[8,136,512]{2,1,0:T(8,128)(2,1)}, u32[]{:S(2)}, u32[]{:S(2)}) collective-permute-start(bf16[8,136,512]{2,1,0:T(8,128)(2,1)S(1)} %all-to-all-done.1.own), channel_id=1, source_target_pairs={{0,16},{16,0},{1,17},{17,1},{2,18},{18,2},{3,19},{19,3},{4,20},{20... | collective-permute-start | bytes 3342344 | tf_op jit(solution)/shard_map/ppermute | solution.py:296
  63.9 20.4 %all-to-all-start.2 = ((bf16[4,8,32,512]{3,2,1,0:T(8,128)(2,1)}), bf16[4,8,32,512]{3,2,1,0:T(8,128)(2,1)}, u32[]{:S(2)}, u32[]{:S(2)}) async-start(bf16[4,8,32,512]{3,2,1,0:T(8,128)(2,1)} %add_convert_fusion), calls=%async_computation.2 | async-start | bytes 2097152 | tf_op jit(solution)/shard_map/all_to_all | solution.py:300
  72.5 17.1 %collective-permute-start.3 = (bf16[4,64,512]{2,1,0:T(8,128)(2,1)}, bf16[4,64,512]{2,1,0:T(8,128)(2,1)}, u32[]{:S(2)}, u32[]{:S(2)}) collective-permute-start(bf16[4,64,512]{2,1,0:T(8,128)(2,1)} %get-tuple-element.39), channel_id=1, source_target_pairs={{0,8},{8,0},{1,9},{9,1},{2,10},{10,2},{3,11},{11,3},{4,12},{12,4},... | collective-permute-start | bytes 786440 | tf_op jit(solution)/shard_map/ppermute | solution.py:296
  78.2 10.3 %collective-permute-start.4 = (bf16[4,64,512]{2,1,0:T(8,128)(2,1)}, bf16[4,64,512]{2,1,0:T(8,128)(2,1)S(1)}, u32[]{:S(2)}, u32[]{:S(2)}) collective-permute-start(bf16[4,64,512]{2,1,0:T(8,128)(2,1)} %get-tuple-element.41), channel_id=1, source_target_pairs={{0,8},{8,0},{1,9},{9,1},{2,10},{10,2},{3,11},{11,3},{4,12},{12,4},... | collective-permute-start | bytes 786440 | tf_op jit(solution)/shard_map/ppermute | solution.py:296
  123.6 5.6 %collective-permute-start.5 = (bf16[40,512]{1,0:T(8,128)(2,1)S(1)}, bf16[40,512]{1,0:T(8,128)(2,1)S(1)}, u32[]{:S(2)}, u32[]{:S(2)}) collective-permute-start(bf16[40,512]{1,0:T(8,128)(2,1)S(1)} %get-tuple-element.50), channel_id=1, source_target_pairs={{0,8},{8,0},{1,9},{9,1},{2,10},{10,2},{3,11},{11,3},{4,12},{12,4},... | collective-permute-start | bytes 122888 | tf_op jit(solution)/shard_map/ppermute | solution.py:296
  125.9 3.9 %collective-permute-start.6 = (bf16[32,512]{1,0:T(8,128)(2,1)S(1)}, bf16[32,512]{1,0:T(8,128)(2,1)S(1)}, u32[]{:S(2)}, u32[]{:S(2)}) collective-permute-start(bf16[32,512]{1,0:T(8,128)(2,1)S(1)} %slice.62), channel_id=1, source_target_pairs={{0,128},{128,0},{1,129},{129,1},{2,130},{130,2},{3,131},{131,3},{4... | collective-permute-start | bytes 98312 | tf_op jit(solution)/shard_map/ppermute | solution.py:296
  126.4 3.9 %collective-permute-start.7 = (bf16[32,512]{1,0:T(8,128)(2,1)S(1)}, bf16[32,512]{1,0:T(8,128)(2,1)S(1)}, u32[]{:S(2)}, u32[]{:S(2)}) collective-permute-start(bf16[32,512]{1,0:T(8,128)(2,1)S(1)} %slice.62), channel_id=1, source_target_pairs={{0,136},{8,128},{128,8},{136,0},{1,137},{9,129},{129,9},{137,1},{2... | collective-permute-start | bytes 98312 | tf_op jit(solution)/shard_map/ppermute | solution.py:360
  154.5 14.1 %collective-permute-start.15 = (bf16[8,64,512]{2,1,0:T(8,128)(2,1)S(1)}, bf16[8,64,512]{2,1,0:T(8,128)(2,1)S(1)}, u32[]{:S(2)}, u32[]{:S(2)}) collective-permute-start(bf16[8,64,512]{2,1,0:T(8,128)(2,1)S(1)} %slice.69), channel_id=1, source_target_pairs={{0,8},{8,0},{1,9},{9,1},{2,10},{10,2},{3,11},{11,3},{4,12},{12,4},... | collective-permute-start | bytes 1572872 | tf_op jit(solution)/shard_map/ppermute | solution.py:296
  157.0 7.7 %collective-permute-start.8 = (bf16[8,32,512]{2,1,0:T(8,128)(2,1)S(1)}, bf16[8,32,512]{2,1,0:T(8,128)(2,1)S(1)}, u32[]{:S(2)}, u32[]{:S(2)}) collective-permute-start(bf16[8,32,512]{2,1,0:T(8,128)(2,1)S(1)} %slice.67.refs_0_), channel_id=1, source_target_pairs={{0,32},{32,64},{64,96},{96,0},{1,33},{33,65},{65,97},{97,1},{2,34}... | collective-permute-start | bytes 786440 | tf_op jit(solution)/shard_map/ppermute | solution.py:309
  158.2 9.8 %collective-permute-start.9 = (bf16[8,32,512]{2,1,0:T(8,128)(2,1)S(1)}, bf16[8,32,512]{2,1,0:T(8,128)(2,1)S(1)}, u32[]{:S(2)}, u32[]{:S(2)}) collective-permute-start(bf16[8,32,512]{2,1,0:T(8,128)(2,1)S(1)} %slice.67.refs_0_), channel_id=1, source_target_pairs={{0,64},{32,96},{64,0},{96,32},{1,65},{33,97},{65,1},{97,33},{2,66}... | collective-permute-start | bytes 786440 | tf_op jit(solution)/shard_map/ppermute | solution.py:309
  160.9 7.3 %collective-permute-start.10 = (bf16[8,32,512]{2,1,0:T(8,128)(2,1)S(1)}, bf16[8,32,512]{2,1,0:T(8,128)(2,1)S(1)}, u32[]{:S(2)}, u32[]{:S(2)}) collective-permute-start(bf16[8,32,512]{2,1,0:T(8,128)(2,1)S(1)} %slice.67.refs_0_), channel_id=1, source_target_pairs={{0,96},{32,0},{64,32},{96,64},{1,97},{33,1},{65,33},{97,65},{2,98}... | collective-permute-start | bytes 786440 | tf_op jit(solution)/shard_map/ppermute | solution.py:309
  162.4 7.5 %collective-permute-start.11 = (bf16[8,32,512]{2,1,0:T(8,128)(2,1)S(1)}, bf16[8,32,512]{2,1,0:T(8,128)(2,1)S(1)}, u32[]{:S(2)}, u32[]{:S(2)}) collective-permute-start(bf16[8,32,512]{2,1,0:T(8,128)(2,1)S(1)} %slice.67.refs_0_), channel_id=1, source_target_pairs={{0,16},{16,0},{1,17},{17,1},{2,18},{18,2},{3,19},{19,3},{4,20},{20... | collective-permute-start | bytes 786440 | tf_op jit(solution)/shard_map/ppermute | solution.py:296
  164.6 5.2 %collective-permute-start.12 = (bf16[8,32,512]{2,1,0:T(8,128)(2,1)S(1)}, bf16[8,32,512]{2,1,0:T(8,128)(2,1)S(1)}, u32[]{:S(2)}, u32[]{:S(2)}) collective-permute-start(bf16[8,32,512]{2,1,0:T(8,128)(2,1)S(1)} %collective-permute-done.8.refs_1_), channel_id=1, source_target_pairs={{0,16},{16,0},{1,17},{17,1},{2,18},{18,2},{3,19},{19,3},{4,20},{20... | collective-permute-start | bytes 786440 | tf_op jit(solution)/shard_map/ppermute | solution.py:296
  168.1 1.8 %collective-permute-start.13 = (bf16[8,32,512]{2,1,0:T(8,128)(2,1)S(1)}, bf16[8,32,512]{2,1,0:T(8,128)(2,1)S(1)}, u32[]{:S(2)}, u32[]{:S(2)}) collective-permute-start(bf16[8,32,512]{2,1,0:T(8,128)(2,1)S(1)} %collective-permute-done.9.refs_2_), channel_id=1, source_target_pairs={{0,16},{16,0},{1,17},{17,1},{2,18},{18,2},{3,19},{19,3},{4,20},{20... | collective-permute-start | bytes 786440 | tf_op jit(solution)/shard_map/ppermute | solution.py:296
  168.3 1.7 collective-permute-start.14
  (1 other events, 0.7 us)
where the time goes:
time: 175 us; the launch traced here: 172 us
  blocking collectives  77.7 us (44%)
  waiting for transfers between devices  28.1 us (16%)
  Pallas kernels  25.9 us (15%)
  starting transfers between devices  23.8 us (14%)
  other arithmetic  7.93 us (5%)
  local copies, waits for them, and re-layouts  7.64 us (4%)
    all_to_all x3, blocking collectives, exchange(): return lax.all_to_all(pieces, axes, split_axis=0, concat_axis=0, tiled=True)  77.7 us
    all_to_all x2, waiting for transfers between devices, exchange(): return lax.all_to_all(pieces, axes, split_axis=0, concat_axis=0, tiled=True)  14.6 us
    pallas_call x1, Pallas kernels, forward(): pl.pallas_call(forward_kernel, in_specs=[SMEM, HBM, HBM, HBM], out_specs=...  9.48 us
    ppermute x12, starting transfers between devices, swap(): return lax.ppermute(x, axis, [(0, 1), (1, 0)])  9.1 us
    pallas_call x2, Pallas kernels, relations_grad(): pl.pallas_call(functools.partial(relations_kernel, first), in_specs=[SMEM...  8.32 us
    all_to_all x2, starting transfers between devices, exchange(): return lax.all_to_all(pieces, axes, split_axis=0, concat_axis=0, tiled=True)  7.99 us
    ppermute x12, waiting for transfers between devices, swap(): return lax.ppermute(x, axis, [(0, 1), (1, 0)])  7.66 us
    ppermute x3, starting transfers between devices, to_x(): return lax.ppermute(x, 'fx', [(i, (i + k) % 4) for i in range(4)])  5.41 us
  transfers between devices with their start and end apart: 18, of which 11 were waited for; matrix products, arithmetic and copies ran while one was open for 7% of the time, Pallas kernels for 5%

commit v1 on v0

--- a/solution.py
+++ b/solution.py
@@ -317,6 +317,12 @@
     return x.astype(F32).sum(axis=0)
 
 
+def two_rows(x):
+    high = x.astype(BF16)
+    low = (x - high.astype(F32)).astype(BF16)
+    return jnp.concatenate([high, low, jnp.zeros((6, D), BF16)], axis=0)
+
+
 def after(x, first):
     return lax.optimization_barrier((x, first))[0]
 
@@ -344,26 +350,25 @@
     keep, send, gains = relations_grad(0, table, own, other, turned)
     got = swap(send, "by")
     keep2, send2, _ = relations_grad(NREL // 2, table, own, other, turned)
-    rel_terms = jnp.concatenate([added(keep, got), added(keep2, swap(send2, "by"))], axis=0)
+    first_half = added(keep, got)
+    got = swap(send2, "by")
+    rel_terms = jnp.concatenate([first_half, added(keep2, got)], axis=0)
 
     terms = summed(after(terms, keep2)).astype(BF16)
-    gain = gains[0:1] + gains[1:2]
-    high = gain.astype(BF16)
-    low = (gain - high.astype(F32)).astype(BF16)
-    gain_rows = jnp.concatenate([high, low, jnp.zeros((6, D), BF16)], axis=0)
-    gain_rows = jnp.broadcast_to(gain_rows[None], (8, 8, D))
-
-    piece = summed(exchange(jnp.concatenate([rel_terms, terms, gain_rows], axis=1), "bz")).astype(BF16)
-    aside = piece[HALF:]
+    rel_terms, gain_rows = lax.optimization_barrier((rel_terms, two_rows(gains[0:1] + gains[1:2])))
+
+    piece = summed(exchange(jnp.concatenate([rel_terms, terms], axis=1), "bz")).astype(BF16)
+    aside = jnp.concatenate([piece[HALF:], gain_rows], axis=0)
     partner = swap(aside, "by").astype(F32)
     beside = swap(aside[:32], "fy").astype(F32)
     across = lax.ppermute(aside[:32], ("fy", "by"), [(i, 3 - i) for i in range(4)]).astype(F32)
     aside = aside.astype(F32)
     term = (aside[:32] + partner[:32]) + (beside + across)
-    gain = aside[32:] + partner[32:]
-    gain = jnp.broadcast_to(gain[0:1] + gain[1:2], (8, D))
-    rows = gather(jnp.concatenate([piece[:HALF], term.astype(BF16), gain.astype(BF16)], axis=0), "bz")
-    grad_gain = rows[0, HALF + 32]
+    gain = aside[32:34] + partner[32:34]
+    gain_rows = two_rows(gain[0:1] + gain[1:2])
+    rows = gather(jnp.concatenate([piece[:HALF], term.astype(BF16), gain_rows], axis=0), "bz")
+    gains = summed(rows[:, HALF + 32 : HALF + 34])
+    grad_gain = (gains[0] + gains[1]).astype(BF16)
     terms = rows[:, HALF : HALF + 32]
 
     piece = rows[:, :HALF]

time: 175 us -> 173 us (0.989)
  no operation moved by 1% of the time
where the time goes in v1:
time: 173 us; the launch traced here: 170 us
  blocking collectives  76 us (44%)
  waiting for transfers between devices  28.1 us (16%)
  Pallas kernels  25.9 us (15%)
  starting transfers between devices  23.9 us (14%)
  other arithmetic  8.49 us (5%)
  local copies, waits for them, and re-layouts  6.98 us (4%)
    all_to_all x3, blocking collectives, exchange(): return lax.all_to_all(pieces, axes, split_axis=0, concat_axis=0, tiled=True)  76 us
    all_to_all x2, waiting for transfers between devices, exchange(): return lax.all_to_all(pieces, axes, split_axis=0, concat_axis=0, tiled=True)  14.8 us
    pallas_call x1, Pallas kernels, forward(): pl.pallas_call(forward_kernel, in_specs=[SMEM, HBM, HBM, HBM], out_specs=...  9.48 us
    ppermute x12, starting transfers between devices, swap(): return lax.ppermute(x, axis, [(0, 1), (1, 0)])  9.1 us
    pallas_call x2, Pallas kernels, relations_grad(): pl.pallas_call(functools.partial(relations_kernel, first), in_specs=[SMEM...  8.32 us
    all_to_all x2, starting transfers between devices, exchange(): return lax.all_to_all(pieces, axes, split_axis=0, concat_axis=0, tiled=True)  7.98 us
    ppermute x12, waiting for transfers between devices, swap(): return lax.ppermute(x, axis, [(0, 1), (1, 0)])  7.55 us
    ppermute x3, starting transfers between devices, to_x(): return lax.ppermute(x, 'fx', [(i, (i + k) % 4) for i in range(4)])  5.45 us
  transfers between devices with their start and end apart: 18, of which 11 were waited for; matrix products, arithmetic and copies ran while one was open for 7% of the time, Pallas kernels for 5%

profile of v1, /device:TPU:16, one launch (start us, length us, event | category | flops | bytes accessed | tf_op | source)
XLA Modules:
  0.0 170.3 jit_solution(6121211275619977362)
XLA Ops:
  1.4 9.5 %forward.1 = (bf16[4,8,128,256]{3,2,1,0:T(8,128)(2,1)}, bf16[8,128,512]{2,1,0:T(8,128)(2,1)S(1)}, bf16[8,128,512]{2,1,0:T(8,128)(2,1)S(1)}) custom-call(s32[5,16]{1,0:T(8,128)S(1)} %pad_add_fusion.table, bf16[8192,256]{1,0:T(8,128)(2,1)} %feats.1, bf16[512,1024]{1,0:T(8,128)(2,1)} %bitcast.20, bf16[4,256,512]{2,1,0:T(8,128)(2,1)} %weight.1), custom_call_target="tpu_custom_call" | custom-call | flops 3221225472 | bytes 10485760 | tf_op jit(solution)/shard_map/forward/pallas_call | solution.py:78
  11.0 2.6 %collective-permute-done = bf16[8,128,512]{2,1,0:T(8,128)(2,1)S(1)} collective-permute-done((bf16[8,128,512]{2,1,0:T(8,128)(2,1)S(1)}, bf16[8,128,512]{2,1,0:T(8,128)(2,1)S(1)}, u32[]{:S(2)}, u32[]{:S(2)}) %collective-permute-start) | collective-permute-done | bytes 1048608 | tf_op jit(solution)/shard_map/ppermute | solution.py:296
  13.9 20.9 %all_to_all.25.arrived = bf16[8,128,512]{2,1,0:T(8,128)(2,1)S(1)} all-to-all(bf16[8,128,512]{2,1,0:T(8,128)(2,1)S(1)} %add_convert_fusion.1), channel_id=1, replica_groups=mesh['fy'=2,'fx'=4,'fc'=2,'by'=2,'bz'=8] {'fy','fx'}, dimensions={0} | all-to-all | bytes 2097152 | tf_op jit(solution)/shard_map/all_to_all | solution.py:300
  34.9 3.6 %layer.1 = (bf16[128,512]{1,0:T(8,128)(2,1)}, bf16[136,512]{1,0:T(8,128)(2,1)S(1)}, bf16[128,512]{1,0:T(8,128)(2,1)S(1)}, bf16[128,1536]{1,0:T(8,128)(2,1)S(1)}, bf16[128,512]{1,0:T(8,128)(2,1)S(1)}) custom-call(bf16[8,128,512]{2,1,0:T(8,128)(2,1)S(1)} %all_to_all.25.arrived, s32[1,128]{1,0:T(1,128)S(1)} %bitcast.15, f32[1,512]{1,0:T(1,128)S(1)} %bitcast.14, ...), custom_call_target="tpu_custom_call" | custom-call | flops 1073741824 | bytes 8388608 | tf_op jit(solution)/shard_map/layer/pallas_call | solution.py:176
  38.5 2.4 %terms.1 = (bf16[4,8,32,512]{3,2,1,0:T(8,128)(2,1)S(1)}, bf16[4,8,32,512]{3,2,1,0:T(8,128)(2,1)}) custom-call(s32[5,16]{1,0:T(8,128)S(1)} %pad_add_fusion.table, bf16[128,512]{1,0:T(8,128)(2,1)S(1)} %get-tuple-element.32.normed, bf16[128,1536]{1,0:T(8,128)(2,1)S(1)} %get-tuple-element.33.d_projected, bf16[128,512]{1,0:T(8,128)(2,1)S(1)} %get-tuple-element.34.context, ...), custom_call_target="tpu_custom_call" | custom-call | flops 268435456 | bytes 5242880 | tf_op jit(solution)/shard_map/terms/pallas_call | solution.py:208
  43.0 3.6 %all-to-all-start.1 = ((bf16[8,136,512]{2,1,0:T(8,128)(2,1)}), bf16[8,136,512]{2,1,0:T(8,128)(2,1)S(1)}, u32[]{:S(2)}, u32[]{:S(2)}) async-start(bf16[8,136,512]{2,1,0:T(8,128)(2,1)} %broadcast_in_dim.27), calls=%async_computation.1 | async-start | bytes 2228224 | tf_op jit(solution)/shard_map/all_to_all | solution.py:300
  46.6 3.0 %copy.18 = bf16[4,1024,256]{1,2,0:T(8,128)(2,1)S(1)} copy(bf16[4,1024,256]{2,1,0:T(8,128)(2,1)} %bitcast.16) | data formatting | bytes 4194304 | tf_op jit(solution)/shard_map/reshape | solution.py:346
  49.6 2.9 %add_convert_fusion = bf16[4,8,32,512]{3,2,1,0:T(8,128)(2,1)} fusion(bf16[4,8,32,512]{3,2,1,0:T(8,128)(2,1)} %collective-permute-done.1, bf16[4,8,32,512]{3,2,1,0:T(8,128)(2,1)} %copy-done), kind=kLoop, calls=%fused_computation | loop fusion | flops 2097152 | bytes 3145728 | tf_op jit(solution)/shard_map/convert_element_type | solution.py:313
  52.5 11.3 %all-to-all-done.1.own = bf16[8,136,512]{2,1,0:T(8,128)(2,1)S(1)} async-done(((bf16[8,136,512]{2,1,0:T(8,128)(2,1)}), bf16[8,136,512]{2,1,0:T(8,128)(2,1)S(1)}, u32[]{:S(2)}, u32[]{:S(2)}) %all-to-all-start.1) | async-done | bytes 1114144 | tf_op jit(solution)/shard_map/all_to_all | solution.py:300
  63.9 4.4 %all-to-all-start.2 = ((bf16[4,8,32,512]{3,2,1,0:T(8,128)(2,1)}), bf16[4,8,32,512]{3,2,1,0:T(8,128)(2,1)}, u32[]{:S(2)}, u32[]{:S(2)}) async-start(bf16[4,8,32,512]{3,2,1,0:T(8,128)(2,1)} %add_convert_fusion), calls=%async_computation.2 | async-start | bytes 2097152 | tf_op jit(solution)/shard_map/all_to_all | solution.py:300
  68.3 4.1 %relations.2 = (bf16[4,64,512]{2,1,0:T(8,128)(2,1)S(1)}, bf16[4,64,512]{2,1,0:T(8,128)(2,1)}, f32[8,512]{1,0:T(8,128)S(1)}) custom-call(s32[5,16]{1,0:T(8,128)S(1)} %pad_add_fusion.table, bf16[8,136,512]{2,1,0:T(8,128)(2,1)S(1)} %all-to-all-done.1.own, bf16[8,136,512]{2,1,0:T(8,128)(2,1)} %collective-permute-done.2.other, bf16[4,256,1024]{2,1,0:T(8,128)(2,1)S(1)} %bitcast.12), custom_call_target="tpu_custom_call" | custom-call | flops 536870912 | bytes 6291456 | tf_op jit(solution)/shard_map/relations/pallas_call | solution.py:254
  73.1 4.2 %relations.3 = (bf16[4,64,512]{2,1,0:T(8,128)(2,1)S(1)}, bf16[4,64,512]{2,1,0:T(8,128)(2,1)}, f32[8,512]{1,0:T(8,128)}) custom-call(s32[5,16]{1,0:T(8,128)S(1)} %pad_add_fusion.table, bf16[8,136,512]{2,1,0:T(8,128)(2,1)S(1)} %all-to-all-done.1.own, bf16[8,136,512]{2,1,0:T(8,128)(2,1)} %collective-permute-done.2.other, bf16[4,256,1024]{2,1,0:T(8,128)(2,1)S(1)} %bitcast.13), custom_call_target="tpu_custom_call" | custom-call | flops 536870912 | bytes 6291456 | tf_op jit(solution)/shard_map/relations/pallas_call | solution.py:254
  78.1 2.7 %collective-permute-start.4 = (bf16[4,64,512]{2,1,0:T(8,128)(2,1)}, bf16[4,64,512]{2,1,0:T(8,128)(2,1)S(1)}, u32[]{:S(2)}, u32[]{:S(2)}) collective-permute-start(bf16[4,64,512]{2,1,0:T(8,128)(2,1)} %get-tuple-element.43), channel_id=1, source_target_pairs={{0,8},{8,0},{1,9},{9,1},{2,10},{10,2},{3,11},{11,3},{4,12},{12,4},... | collective-permute-start | bytes 786440 | tf_op jit(solution)/shard_map/ppermute | solution.py:296
  80.8 3.4 %all-to-all-done.2 = bf16[4,8,32,512]{3,2,1,0:T(8,128)(2,1)} async-done(((bf16[4,8,32,512]{3,2,1,0:T(8,128)(2,1)}), bf16[4,8,32,512]{3,2,1,0:T(8,128)(2,1)}, u32[]{:S(2)}, u32[]{:S(2)}) %all-to-all-start.2) | async-done | bytes 1048608 | tf_op jit(solution)/shard_map/all_to_all | solution.py:300
  85.6 2.8 %collective-permute-done.4 = bf16[4,64,512]{2,1,0:T(8,128)(2,1)S(1)} collective-permute-done((bf16[4,64,512]{2,1,0:T(8,128)(2,1)}, bf16[4,64,512]{2,1,0:T(8,128)(2,1)S(1)}, u32[]{:S(2)}, u32[]{:S(2)}) %collective-permute-start.4) | collective-permute-done | bytes 262176 | tf_op jit(solution)/shard_map/ppermute | solution.py:296
  90.6 31.3 %all_to_all.26 = bf16[8,96,512]{2,1,0:T(8,128)(2,1)S(1)} all-to-all(bf16[8,96,512]{2,1,0:T(8,128)(2,1)S(1)} %pad_maximum_fusion.1), channel_id=1, replica_groups=mesh['fy'=2,'fx'=4,'fc'=2,'by'=2,'bz'=8] {'bz'}, dimensions={0} | all-to-all | bytes 1572864 | tf_op jit(solution)/shard_map/all_to_all | solution.py:300
  122.1 2.3 %collective-permute-start.5 = (bf16[40,512]{1,0:T(8,128)(2,1)S(1)}, bf16[40,512]{1,0:T(8,128)(2,1)S(1)}, u32[]{:S(2)}, u32[]{:S(2)}) collective-permute-start(bf16[40,512]{1,0:T(8,128)(2,1)S(1)} %get-tuple-element.54), channel_id=1, source_target_pairs={{0,8},{8,0},{1,9},{9,1},{2,10},{10,2},{3,11},{11,3},{4,12},{12,4},... | collective-permute-start | bytes 122888 | tf_op jit(solution)/shard_map/ppermute | solution.py:296
  128.9 23.7 %all_to_all.27 = bf16[8,104,512]{2,1,0:T(8,128)(2,1)S(1)} all-to-all(bf16[8,104,512]{2,1,0:T(8,128)(2,1)S(1)} %broadcast_in_dim.28), channel_id=1, replica_groups=mesh['fy'=2,'fx'=4,'fc'=2,'by'=2,'bz'=8] {'bz'}, dimensions={0} | all-to-all | bytes 1703936 | tf_op jit(solution)/shard_map/all_to_all | solution.py:300
  152.7 2.5 %collective-permute-start.15 = (bf16[8,64,512]{2,1,0:T(8,128)(2,1)S(1)}, bf16[8,64,512]{2,1,0:T(8,128)(2,1)S(1)}, u32[]{:S(2)}, u32[]{:S(2)}) collective-permute-start(bf16[8,64,512]{2,1,0:T(8,128)(2,1)S(1)} %slice.72), channel_id=1, source_target_pairs={{0,8},{8,0},{1,9},{9,1},{2,10},{10,2},{3,11},{11,3},{4,12},{12,4},... | collective-permute-start | bytes 1572872 | tf_op jit(solution)/shard_map/ppermute | solution.py:296
  156.5 2.7 %collective-permute-start.9 = (bf16[8,32,512]{2,1,0:T(8,128)(2,1)S(1)}, bf16[8,32,512]{2,1,0:T(8,128)(2,1)S(1)}, u32[]{:S(2)}, u32[]{:S(2)}) collective-permute-start(bf16[8,32,512]{2,1,0:T(8,128)(2,1)S(1)} %slice.68.refs_0_), channel_id=1, source_target_pairs={{0,64},{32,96},{64,0},{96,32},{1,65},{33,97},{65,1},{97,33},{2,66}... | collective-permute-start | bytes 786440 | tf_op jit(solution)/shard_map/ppermute | solution.py:309
  159.2 1.5 collective-permute-start.10
  161.3 1.7 collective-permute-done.8.refs_1_
  162.9 3.4 %collective-permute-done.9.refs_2_ = bf16[8,32,512]{2,1,0:T(8,128)(2,1)S(1)} collective-permute-done((bf16[8,32,512]{2,1,0:T(8,128)(2,1)S(1)}, bf16[8,32,512]{2,1,0:T(8,128)(2,1)S(1)}, u32[]{:S(2)}, u32[]{:S(2)}) %collective-permute-start.9) | collective-permute-done | bytes 262176 | tf_op jit(solution)/shard_map/ppermute | solution.py:309
  168.2 2.1 %assemble.1 = (bf16[512,1536]{1,0:T(8,128)(2,1)}, bf16[512,512]{1,0:T(8,128)(2,1)}) custom-call(s32[5,16]{1,0:T(8,128)S(1)} %pad_add_fusion.table, bf16[8,32,512]{2,1,0:T(8,128)(2,1)S(1)} %slice.68.refs_0_, bf16[8,32,512]{2,1,0:T(8,128)(2,1)S(1)} %collective-permute-done.8.refs_1_, bf16[8,32,512]{2,1,0:T(8,128)(2,1)S(1)} %collective-permute-done.9.refs_2_, ...), custom_call_target="tpu_custom_call" | custom-call | bytes 4194304 | tf_op jit(solution)/shard_map/assemble/pallas_call | solution.py:284
  (66 shorter events, 16.7 us)
Async XLA Ops:
  10.8 2.7 %collective-permute-start = (bf16[8,128,512]{2,1,0:T(8,128)(2,1)S(1)}, bf16[8,128,512]{2,1,0:T(8,128)(2,1)S(1)}, u32[]{:S(2)}, u32[]{:S(2)}) collective-permute-start(bf16[8,128,512]{2,1,0:T(8,128)(2,1)S(1)} %get-tuple-element.29), channel_id=1, source_target_pairs={{0,16},{16,0},{1,17},{17,1},{2,18},{18,2},{3,19},{19,3},{4,20},{20... | collective-permute-start | bytes 3145736 | tf_op jit(solution)/shard_map/ppermute | solution.py:296
  13.6 21.3 %copy-start.2 = (bf16[512,1536]{1,0:T(8,128)(2,1)S(1)}, bf16[512,1536]{1,0:T(8,128)(2,1)}, u32[]{:S(2)}) copy-start(bf16[512,1536]{1,0:T(8,128)(2,1)} %w_qkv.1) | copy-start | bytes 4718596
  13.6 21.3 %copy-start.3 = (bf16[512,512]{1,0:T(8,128)(2,1)S(1)}, bf16[512,512]{1,0:T(8,128)(2,1)}, u32[]{:S(2)}) copy-start(bf16[512,512]{1,0:T(8,128)(2,1)} %w_out.1) | copy-start | bytes 1572868
  13.6 21.3 %copy-start.4 = (bf16[128,512]{1,0:T(8,128)(2,1)S(1)}, bf16[128,512]{1,0:T(8,128)(2,1)}, u32[]{:S(2)}) copy-start(bf16[128,512]{1,0:T(8,128)(2,1)} %cot.3) | copy-start | bytes 393220
  13.6 21.3 %copy-start.5 = (f32[512]{0:T(512)S(1)}, f32[512]{0:T(512)}, u32[]{:S(2)}) copy-start(f32[512]{0:T(512)} %param.16) | copy-start | bytes 6148
  13.6 21.3 %copy-start.6 = (s32[128]{0:T(128)S(1)}, s32[128]{0:T(128)}, u32[]{:S(2)}) copy-start(s32[128]{0:T(128)} %param.13) | copy-start | bytes 1540
  41.0 1.0 copy-start
  41.9 7.6 %collective-permute-start.1 = (bf16[4,8,32,512]{3,2,1,0:T(8,128)(2,1)}, bf16[4,8,32,512]{3,2,1,0:T(8,128)(2,1)}, u32[]{:S(2)}, u32[]{:S(2)}) collective-permute-start(bf16[4,8,32,512]{3,2,1,0:T(8,128)(2,1)} %get-tuple-element.36), channel_id=1, source_target_pairs={{0,16},{16,0},{1,17},{17,1},{2,18},{18,2},{3,19},{19,3},{4,20},{20... | collective-permute-start | bytes 3145736 | tf_op jit(solution)/shard_map/ppermute | solution.py:296
  43.0 20.9 %all-to-all-start.1 = ((bf16[8,136,512]{2,1,0:T(8,128)(2,1)}), bf16[8,136,512]{2,1,0:T(8,128)(2,1)S(1)}, u32[]{:S(2)}, u32[]{:S(2)}) async-start(bf16[8,136,512]{2,1,0:T(8,128)(2,1)} %broadcast_in_dim.27), calls=%async_computation.1 | async-start | bytes 2228224 | tf_op jit(solution)/shard_map/all_to_all | solution.py:300
  63.9 4.4 %collective-permute-start.2 = (bf16[8,136,512]{2,1,0:T(8,128)(2,1)S(1)}, bf16[8,136,512]{2,1,0:T(8,128)(2,1)}, u32[]{:S(2)}, u32[]{:S(2)}) collective-permute-start(bf16[8,136,512]{2,1,0:T(8,128)(2,1)S(1)} %all-to-all-done.1.own), channel_id=1, source_target_pairs={{0,16},{16,0},{1,17},{17,1},{2,18},{18,2},{3,19},{19,3},{4,20},{20... | collective-permute-start | bytes 3342344 | tf_op jit(solution)/shard_map/ppermute | solution.py:296
  63.9 20.4 %all-to-all-start.2 = ((bf16[4,8,32,512]{3,2,1,0:T(8,128)(2,1)}), bf16[4,8,32,512]{3,2,1,0:T(8,128)(2,1)}, u32[]{:S(2)}, u32[]{:S(2)}) async-start(bf16[4,8,32,512]{3,2,1,0:T(8,128)(2,1)} %add_convert_fusion), calls=%async_computation.2 | async-start | bytes 2097152 | tf_op jit(solution)/shard_map/all_to_all | solution.py:300
  72.4 17.1 %collective-permute-start.3 = (bf16[4,64,512]{2,1,0:T(8,128)(2,1)}, bf16[4,64,512]{2,1,0:T(8,128)(2,1)}, u32[]{:S(2)}, u32[]{:S(2)}) collective-permute-start(bf16[4,64,512]{2,1,0:T(8,128)(2,1)} %get-tuple-element.41), channel_id=1, source_target_pairs={{0,8},{8,0},{1,9},{9,1},{2,10},{10,2},{3,11},{11,3},{4,12},{12,4},... | collective-permute-start | bytes 786440 | tf_op jit(solution)/shard_map/ppermute | solution.py:296
  78.1 10.3 %collective-permute-start.4 = (bf16[4,64,512]{2,1,0:T(8,128)(2,1)}, bf16[4,64,512]{2,1,0:T(8,128)(2,1)S(1)}, u32[]{:S(2)}, u32[]{:S(2)}) collective-permute-start(bf16[4,64,512]{2,1,0:T(8,128)(2,1)} %get-tuple-element.43), channel_id=1, source_target_pairs={{0,8},{8,0},{1,9},{9,1},{2,10},{10,2},{3,11},{11,3},{4,12},{12,4},... | collective-permute-start | bytes 786440 | tf_op jit(solution)/shard_map/ppermute | solution.py:296
  122.1 5.6 %collective-permute-start.5 = (bf16[40,512]{1,0:T(8,128)(2,1)S(1)}, bf16[40,512]{1,0:T(8,128)(2,1)S(1)}, u32[]{:S(2)}, u32[]{:S(2)}) collective-permute-start(bf16[40,512]{1,0:T(8,128)(2,1)S(1)} %get-tuple-element.54), channel_id=1, source_target_pairs={{0,8},{8,0},{1,9},{9,1},{2,10},{10,2},{3,11},{11,3},{4,12},{12,4},... | collective-permute-start | bytes 122888 | tf_op jit(solution)/shard_map/ppermute | solution.py:296
  124.4 3.9 %collective-permute-start.6 = (bf16[32,512]{1,0:T(8,128)(2,1)S(1)}, bf16[32,512]{1,0:T(8,128)(2,1)S(1)}, u32[]{:S(2)}, u32[]{:S(2)}) collective-permute-start(bf16[32,512]{1,0:T(8,128)(2,1)S(1)} %slice.61), channel_id=1, source_target_pairs={{0,128},{128,0},{1,129},{129,1},{2,130},{130,2},{3,131},{131,3},{4... | collective-permute-start | bytes 98312 | tf_op jit(solution)/shard_map/ppermute | solution.py:296
  124.9 3.9 %collective-permute-start.7 = (bf16[32,512]{1,0:T(8,128)(2,1)S(1)}, bf16[32,512]{1,0:T(8,128)(2,1)S(1)}, u32[]{:S(2)}, u32[]{:S(2)}) collective-permute-start(bf16[32,512]{1,0:T(8,128)(2,1)S(1)} %slice.61), channel_id=1, source_target_pairs={{0,136},{8,128},{128,8},{136,0},{1,137},{9,129},{129,9},{137,1},{2... | collective-permute-start | bytes 98312 | tf_op jit(solution)/shard_map/ppermute | solution.py:364
  152.7 14.1 %collective-permute-start.15 = (bf16[8,64,512]{2,1,0:T(8,128)(2,1)S(1)}, bf16[8,64,512]{2,1,0:T(8,128)(2,1)S(1)}, u32[]{:S(2)}, u32[]{:S(2)}) collective-permute-start(bf16[8,64,512]{2,1,0:T(8,128)(2,1)S(1)} %slice.72), channel_id=1, source_target_pairs={{0,8},{8,0},{1,9},{9,1},{2,10},{10,2},{3,11},{11,3},{4,12},{12,4},... | collective-permute-start | bytes 1572872 | tf_op jit(solution)/shard_map/ppermute | solution.py:296
  155.2 7.7 %collective-permute-start.8 = (bf16[8,32,512]{2,1,0:T(8,128)(2,1)S(1)}, bf16[8,32,512]{2,1,0:T(8,128)(2,1)S(1)}, u32[]{:S(2)}, u32[]{:S(2)}) collective-permute-start(bf16[8,32,512]{2,1,0:T(8,128)(2,1)S(1)} %slice.68.refs_0_), channel_id=1, source_target_pairs={{0,32},{32,64},{64,96},{96,0},{1,33},{33,65},{65,97},{97,1},{2,34}... | collective-permute-start | bytes 786440 | tf_op jit(solution)/shard_map/ppermute | solution.py:309
  156.5 9.8 %collective-permute-start.9 = (bf16[8,32,512]{2,1,0:T(8,128)(2,1)S(1)}, bf16[8,32,512]{2,1,0:T(8,128)(2,1)S(1)}, u32[]{:S(2)}, u32[]{:S(2)}) collective-permute-start(bf16[8,32,512]{2,1,0:T(8,128)(2,1)S(1)} %slice.68.refs_0_), channel_id=1, source_target_pairs={{0,64},{32,96},{64,0},{96,32},{1,65},{33,97},{65,1},{97,33},{2,66}... | collective-permute-start | bytes 786440 | tf_op jit(solution)/shard_map/ppermute | solution.py:309
  159.2 7.4 %collective-permute-start.10 = (bf16[8,32,512]{2,1,0:T(8,128)(2,1)S(1)}, bf16[8,32,512]{2,1,0:T(8,128)(2,1)S(1)}, u32[]{:S(2)}, u32[]{:S(2)}) collective-permute-start(bf16[8,32,512]{2,1,0:T(8,128)(2,1)S(1)} %slice.68.refs_0_), channel_id=1, source_target_pairs={{0,96},{32,0},{64,32},{96,64},{1,97},{33,1},{65,33},{97,65},{2,98}... | collective-permute-start | bytes 786440 | tf_op jit(solution)/shard_map/ppermute | solution.py:309
  160.6 7.5 %collective-permute-start.11 = (bf16[8,32,512]{2,1,0:T(8,128)(2,1)S(1)}, bf16[8,32,512]{2,1,0:T(8,128)(2,1)S(1)}, u32[]{:S(2)}, u32[]{:S(2)}) collective-permute-start(bf16[8,32,512]{2,1,0:T(8,128)(2,1)S(1)} %slice.68.refs_0_), channel_id=1, source_target_pairs={{0,16},{16,0},{1,17},{17,1},{2,18},{18,2},{3,19},{19,3},{4,20},{20... | collective-permute-start | bytes 786440 | tf_op jit(solution)/shard_map/ppermute | solution.py:296
  162.9 5.2 %collective-permute-start.12 = (bf16[8,32,512]{2,1,0:T(8,128)(2,1)S(1)}, bf16[8,32,512]{2,1,0:T(8,128)(2,1)S(1)}, u32[]{:S(2)}, u32[]{:S(2)}) collective-permute-start(bf16[8,32,512]{2,1,0:T(8,128)(2,1)S(1)} %collective-permute-done.8.refs_1_), channel_id=1, source_target_pairs={{0,16},{16,0},{1,17},{17,1},{2,18},{18,2},{3,19},{19,3},{4,20},{20... | collective-permute-start | bytes 786440 | tf_op jit(solution)/shard_map/ppermute | solution.py:296
  166.3 1.8 %collective-permute-start.13 = (bf16[8,32,512]{2,1,0:T(8,128)(2,1)S(1)}, bf16[8,32,512]{2,1,0:T(8,128)(2,1)S(1)}, u32[]{:S(2)}, u32[]{:S(2)}) collective-permute-start(bf16[8,32,512]{2,1,0:T(8,128)(2,1)S(1)} %collective-permute-done.9.refs_2_), channel_id=1, source_target_pairs={{0,16},{16,0},{1,17},{17,1},{2,18},{18,2},{3,19},{19,3},{4,20},{20... | collective-permute-start | bytes 786440 | tf_op jit(solution)/shard_map/ppermute | solution.py:296
  166.5 1.7 %collective-permute-start.14 = (bf16[8,32,512]{2,1,0:T(8,128)(2,1)S(1)}, bf16[8,32,512]{2,1,0:T(8,128)(2,1)S(1)}, u32[]{:S(2)}, u32[]{:S(2)}) collective-permute-start(bf16[8,32,512]{2,1,0:T(8,128)(2,1)S(1)} %collective-permute-done.10.refs_3_), channel_id=1, source_target_pairs={{0,16},{16,0},{1,17},{17,1},{2,18},{18,2},{3,19},{19,3},{4,20},{20... | collective-permute-start | bytes 786440 | tf_op jit(solution)/shard_map/ppermute | solution.py:296
  (1 other events, 0.7 us)
